TPU v7x, 512 devices: a whole 4x4x16 slice. The times are simulated.
512 devices in a mesh: section: 2 (over core), dp: 64 (over z, y), mp: 4 (over x).
Axes of the slice: x: 4, y: 4, z: 16, core: 2. Of those that a mesh axis runs over, the one named last changes fastest.
Arguments:
- qkv: bfloat16 [8192, 3072], P('dp', ('section', 'mp')), may hold values from -6 to 6
- kv_cache: bfloat16 [4096, 8, 2048], P('dp', None, ('section', 'mp')), may hold values from -6 to 6
- residual: bfloat16 [8192, 2048], P('dp'), may hold values from -6 to 6
- out_weight: bfloat16 [1024, 2048], P(('section', 'mp')), may hold values from -0.1875 to 0.1875
- moe_gain: float32 [2048], replicated, may hold values from 0.1 to 1.9
- w_gate: bfloat16 [64, 2048, 1408], P('dp', None, ('section', 'mp')), may hold values from -0.125 to 0.125
- w_up: bfloat16 [64, 2048, 1408], P('dp', None, ('section', 'mp')), may hold values from -0.125 to 0.125
- w_down: bfloat16 [64, 1408, 2048], P('dp', ('section', 'mp')), may hold values from -0.15625 to 0.15625
- seg_ids: int32 [64, 1, 128], P('dp'), may hold values from 0 to 3, never falling along the last dimension, each value on 1 to 64 neighbouring positions
- prefix_blocks: int32 [64, 1, 4], P('dp'), may hold values from 1 to 32, 64 in all within a row
- owners: int32 [64, 1, 64, 1], replicated, may hold values from 0 to 63; in each aligned block of 64 rows (0 to 63, 64 to 127, ..., all dimensions but the last counted through in order) at most 3 rows name the same one
- slot_ids: int32 [64, 1, 64], replicated, may hold values from 0 to 63
- expert_ids: int32 [8192, 4], P('dp'), may hold values from 0 to 63, all different within a row; in each aligned block of 16 rows (0 to 15, 16 to 31, ...) at most 2 rows name the same one
- gate_weights: float32 [8192, 4], P('dp'), may hold values from 0.05 to 0.5
Outputs:
- layer_out: bfloat16 [8192, 2048], P('dp', ('section', 'mp'))
Inputs may be any that keep to these rules, and one draw needn't show every extreme that they name: seg_ids[g, m] never falls along the tokens; each of the 4 requests has 1 to 64 tokens, one exactly 64. `prefix_blocks`: the 4 counts of each (g, m) sum to 64, one of them is 32. `owners`: in each block table of 64 entries no owner appears more than 3 times, and some owner appears exactly 3 times in some table. `expert_ids`: each token names 4 different experts; in each aligned block of 16 tokens no expert is named by more than 2 tokens, a bound that some block reaches.
All inputs are finite; a program needn't handle non-finite values.
Results may differ from a plain program's by a relative error of at most 0.009.
Values may be sent and summed in bfloat16 or wider, within the bound.
No kernel may reach another device: no remote copies, remote signals or barrier semaphores. Data moves between devices by JAX's collectives and lax.ppermute only.
A program may use at most 64 MiB of HBM per device.

v0:
```python
import math
import jax
import jax.numpy as jnp
from jax import lax
from jax.sharding import PartitionSpec as P

HEAD_DIM = 128
TOPK = 4
PREF = 64
BLK = 8


def normalize(hidden, gain):
    square = jnp.mean(hidden * hidden, axis=-1, keepdims=True)
    return (hidden * lax.rsqrt(square + 1e-06) * gain).astype(jnp.bfloat16)


def expert_rows(inputs, w_gate, w_up, w_down):
    model_width = inputs.shape[-1]
    flat_rows = inputs.reshape(-1, model_width)
    gate_rows = jnp.dot(flat_rows, w_gate[0], preferred_element_type=jnp.float32)
    up_rows = jnp.dot(flat_rows, w_up[0], preferred_element_type=jnp.float32)
    hidden = (jax.nn.silu(gate_rows) * up_rows).astype(jnp.bfloat16)
    result = jnp.dot(hidden, w_down[0], preferred_element_type=jnp.float32).astype(jnp.bfloat16)
    return result.reshape(inputs.shape[:-1] + (result.shape[-1],))


def slot_table(pair_ids, pair_slots, experts, capacity):
    pair_count = pair_ids.shape[0]
    expert_match = pair_ids[None, None, :] == jnp.arange(experts, dtype=jnp.int32)[:, None, None]
    slot_match = pair_slots[None, None, :] == jnp.arange(capacity, dtype=jnp.int32)[None, :, None]
    pair_match = expert_match & slot_match
    token_of = jnp.arange(pair_count, dtype=jnp.int32) // TOPK
    source = jnp.sum(jnp.where(pair_match, token_of[None, None, :], 0), axis=2)
    filled = jnp.any(pair_match, axis=2)
    return (source, filled)


def dispatch_rows(normed, source, filled):
    gathered = jnp.take(normed, source.reshape(-1), axis=0).reshape(
        source.shape + (normed.shape[-1],)
    )
    return jnp.where(filled[:, :, None], gathered, jnp.zeros_like(gathered))


def local(
    qkv,
    kv_cache,
    residual,
    out_weight,
    moe_gain,
    w_gate,
    w_up,
    w_down,
    seg_ids,
    prefix_blocks,
    owners,
    slot_ids,
    expert_ids,
    gate_weights,
):
    groups = lax.axis_size("dp")
    shards = lax.axis_size("section") * lax.axis_size("mp")
    group_index = lax.axis_index("dp")
    shard_index = lax.axis_index("section") * lax.axis_size("mp") + lax.axis_index("mp")
    mb_rows = seg_ids.shape[2]
    quarter_rows = mb_rows // shards
    model_width = residual.shape[1]
    part_cols = model_width // shards
    head_cols = out_weight.shape[0]
    heads_local = head_cols // HEAD_DIM
    cache_cols = kv_cache.shape[2]
    quarter_cap = min(quarter_rows, max(2, 2 * quarter_rows * TOPK // groups))
    capacity = shards * quarter_cap
    owner_cap = max(3, 3 * PREF // groups)
    score_scale = 1.0 / math.sqrt(HEAD_DIM)
    own_table = owners[:, 0, :, 0]
    slot_table_m = slot_ids[:, 0, :]
    owned_here = own_table == group_index
    local_order = jnp.cumsum(owned_here.astype(jnp.int32), axis=1) - 1
    wanted = owned_here[:, None, :] & (
        local_order[:, None, :] == jnp.arange(owner_cap, dtype=jnp.int32)[None, :, None]
    )
    slot_pick = jnp.sum(jnp.where(wanted, slot_table_m[:, None, :], 0), axis=2)
    filled = jnp.any(wanted, axis=2)
    chosen = jnp.take(kv_cache, slot_pick.reshape(-1), axis=0).reshape(
        groups, owner_cap, BLK, cache_cols
    )
    chosen = jnp.where(filled[:, :, None, None], chosen, jnp.zeros_like(chosen))
    arrived = lax.all_to_all(chosen, "dp", split_axis=0, concat_axis=0, tiled=True)
    my_owner = lax.dynamic_index_in_dim(own_table, group_index, 0, keepdims=False)
    block_index = jnp.arange(PREF, dtype=jnp.int32)
    earlier = (my_owner[None, :] == my_owner[:, None]) & (
        block_index[None, :] < block_index[:, None]
    )
    my_rank = jnp.sum(earlier.astype(jnp.int32), axis=1)
    where_from = my_owner * owner_cap + my_rank
    prefix = jnp.take(arrived.reshape(groups * owner_cap, BLK, cache_cols), where_from, axis=0)
    prefix = prefix.reshape(PREF * BLK, heads_local, 2, HEAD_DIM)
    tokens = qkv
    tokens = tokens.reshape(mb_rows, heads_local, 3, HEAD_DIM)
    query_rows = tokens[:, :, 0]
    key_rows = jnp.concatenate([prefix[:, :, 0], tokens[:, :, 1]], axis=0)
    value_rows = jnp.concatenate([prefix[:, :, 1], tokens[:, :, 2]], axis=0)
    segments = seg_ids[0, 0]
    block_ends = jnp.cumsum(prefix_blocks[0, 0])
    block_seg = jnp.sum((block_ends[None, :] <= block_index[:, None]).astype(jnp.int32), axis=1)
    prefix_seg = jnp.repeat(block_seg, BLK)
    position = jnp.arange(mb_rows, dtype=jnp.int32)
    same_prefix = prefix_seg[None, :] == segments[:, None]
    same_new = (segments[None, :] == segments[:, None]) & (position[None, :] <= position[:, None])
    visible = jnp.concatenate([same_prefix, same_new], axis=1)
    scores = (
        jnp.einsum("qhd,khd->hqk", query_rows, key_rows, preferred_element_type=jnp.float32)
        * score_scale
    )
    scores = jnp.where(visible[None], scores, -jnp.inf)
    row_max = jnp.max(scores, axis=2, keepdims=True)
    weights = jnp.exp(scores - row_max)
    attention = (weights / jnp.sum(weights, axis=2, keepdims=True)).astype(jnp.bfloat16)
    combined = jnp.einsum("hqk,khd->qhd", attention, value_rows, preferred_element_type=jnp.float32)
    attended_now = combined.astype(jnp.bfloat16).reshape(mb_rows, head_cols)
    stream = residual.astype(jnp.float32)
    projected = jnp.dot(attended_now, out_weight, preferred_element_type=jnp.float32)
    quarter_ids = expert_ids.reshape(shards, quarter_rows * TOPK)
    one_hot = (
        quarter_ids[:, :, None] == jnp.arange(groups, dtype=jnp.int32)[None, None, :]
    ).astype(jnp.int32)
    quarter_rank = jnp.sum((jnp.cumsum(one_hot, axis=1) - one_hot) * one_hot, axis=2)
    flat_ids = expert_ids.reshape(-1)
    flat_slot = (quarter_rank + jnp.arange(shards, dtype=jnp.int32)[:, None] * quarter_cap).reshape(
        -1
    )
    mixed_in = stream + lax.psum(projected, ("section", "mp"))
    normed = normalize(mixed_in, moe_gain)
    source, filled = slot_table(flat_ids, flat_slot, groups, capacity)
    outgoing = dispatch_rows(normed, source, filled)
    incoming = lax.all_to_all(outgoing, "dp", split_axis=0, concat_axis=0, tiled=True)
    produced = expert_rows(incoming, w_gate, w_up, w_down)
    returned = lax.all_to_all(produced, "dp", split_axis=0, concat_axis=0, tiled=True)
    position = flat_ids * capacity + flat_slot
    picked = jnp.take(returned.reshape(groups * capacity, model_width), position, axis=0)
    picked = picked.reshape(mb_rows, TOPK, model_width)
    weighted = jnp.einsum("tk,tkd->td", gate_weights, picked.astype(jnp.float32))
    moe_full = lax.psum(weighted.astype(jnp.bfloat16), ("section", "mp")).astype(jnp.float32)
    finished = (mixed_in + moe_full).astype(jnp.bfloat16).reshape(mb_rows, shards, part_cols)
    return lax.dynamic_index_in_dim(finished, shard_index, 1, keepdims=False)


def solution(mesh):
    return jax.shard_map(
        local,
        mesh=mesh,
        in_specs=(
            P("dp", ("section", "mp")),
            P("dp", None, ("section", "mp")),
            P("dp", None),
            P(("section", "mp"), None),
            P(),
            P("dp", None, ("section", "mp")),
            P("dp", None, ("section", "mp")),
            P("dp", ("section", "mp"), None),
            P("dp", None, None),
            P("dp", None, None),
            P(),
            P(),
            P("dp", None),
            P("dp", None),
        ),
        out_specs=P("dp", ("section", "mp")),
        check_vma=False,
    )
```

profile of v0, /device:TPU:8, one launch (start us, length us, event | category | flops | bytes accessed | tf_op | source)
XLA Modules:
  0.0 661.5 jit_solution(7814979342064895918)
XLA Ops:
  6.6 0.9 broadcast_compare_fusion.1
  7.4 0.2 reduce_window_sum.29
  7.7 0.9 select_reduce_fusion
  8.6 0.1 copy.73
  8.7 0.2 fusion.36
  8.8 0.1 reshape.389
  9.0 0.1 copy.72
  9.1 0.1 copy.71
  9.2 1.8 gather_fusion
  11.0 1.3 select_select_fusion.1
  12.4 18.7 %all-to-all-start = ((bf16[64,3,8,256]{3,2,1,0:T(8,128)(2,1)}), bf16[64,3,8,256]{3,2,1,0:T(8,128)(2,1)S(1)}, u32[]{:S(2)}, u32[]{:S(2)}) async-start(bf16[64,3,8,256]{3,2,1,0:T(8,128)(2,1)} %select_select_fusion.1), calls=%async_computation | async-start | bytes 1572864 | tf_op jit(solution)/shard_map/all_to_all | solution.py:90
  31.2 0.1 copy.78
  31.3 0.1 eq.143
  31.4 0.1 eq.147
  31.5 0.7 fusion.43
  32.1 0.2 convert_reduce_fusion
  32.3 0.7 compare_and_fusion.3
  33.1 0.1 broadcast_in_dim.123
  33.2 0.1 copy.74
  33.3 0.1 copy.76
  33.4 0.2 reduce-window.8
  33.6 0.1 convert_reduce_fusion.1
  33.8 0.1 eq.135
  33.9 0.1 copy.75
  34.0 0.1 copy.79
  34.1 1.4 fusion.53
  35.7 1.2 fusion
  36.9 0.1 reshape.398
  37.0 0.7 fusion.42
  37.7 0.1 fusion.37
  37.8 0.1 broadcast_compare_fusion
  37.9 37.1 %all-to-all-done = bf16[64,3,8,256]{3,2,1,0:T(8,128)(2,1)S(1)} async-done(((bf16[64,3,8,256]{3,2,1,0:T(8,128)(2,1)}), bf16[64,3,8,256]{3,2,1,0:T(8,128)(2,1)S(1)}, u32[]{:S(2)}, u32[]{:S(2)}) %all-to-all-start) | async-done | bytes 786464 | tf_op jit(solution)/shard_map/all_to_all | solution.py:90
  75.0 0.6 gather_fusion.1
  75.7 1.8 broadcast_select_fusion
  77.5 0.4 fusion.50
  77.9 0.2 fusion.52
  78.1 0.1 fusion.22
  78.3 1.5 fusion.8
  79.8 1.2 and_reduce_fusion
  81.0 68.3 %all-reduce.3.cloned.1.call-done = f32[128,2048]{1,0:T(8,128)} async-done(((f32[128,2048]{1,0:T(8,128)}), f32[128,2048]{1,0:T(8,128)}) %all-reduce.3.cloned.1.call-update) | async-done | bytes 1048592 | tf_op jit(solution)/shard_map/psum | solution.py:134
  149.4 1.4 multiply_reduce_fusion
  150.8 1.4 multiply_convert_fusion
  152.2 6.0 gather_fusion.2
  158.3 2.6 select_select_fusion
  160.8 203.6 %all_to_all.15 = bf16[64,16,2048]{2,1,0:T(8,128)(2,1)S(1)} all-to-all(bf16[64,16,2048]{2,1,0:T(8,128)(2,1)S(1)} %select_select_fusion), channel_id=1, replica_groups=mesh['section'=2,'dp'=64,'mp'=4] {'dp'}, dimensions={0} | all-to-all | bytes 8388608 | tf_op jit(solution)/shard_map/all_to_all | solution.py:138
  364.5 2.0 copy-done.3
  366.5 1.5 fusion.14
  368.0 6.8 %convolution_convert_fusion = bf16[1024,2048]{1,0:T(8,128)(2,1)} fusion(bf16[1024,2048]{1,0:T(8,128)(2,1)} %bitcast.88, bf16[1,176,2048]{2,1,0:T(8,128)(2,1)S(1)} %copy-done, bf16[1,2048,176]{1,2,0:T(8,128)(2,1)S(1)} %copy-done.11, f32[1024,176]{0,1:T(8,128)S(1)} %fusion.14), kind=kOutput, calls=%fused_computation.5 | convolution fusion | flops 1479573504 | bytes 10551296 | tf_op jit(solution)/shard_map/dot_general | solution.py:24
  374.9 6.3 all-to-all-start.2
  381.4 0.1 copy.85
  381.5 0.1 mul.112
  381.7 0.1 add.212
  381.9 0.1 copy.82
  382.0 0.2 copy.87
  382.2 186.9 %all-to-all-done.2 = bf16[64,16,2048]{2,1,0:T(8,128)(2,1)} async-done(((bf16[64,16,2048]{2,1,0:T(8,128)(2,1)}), bf16[64,16,2048]{2,1,0:T(8,128)(2,1)}, u32[]{:S(2)}, u32[]{:S(2)}) %all-to-all-start.2) | async-done | bytes 4194336 | tf_op jit(solution)/shard_map/all_to_all | solution.py:140
  569.1 7.1 %gather_fusion.3 = bf16[512,2048]{1,0:T(8,128)(2,1)S(1)} fusion(bf16[1024,2048]{1,0:T(8,128)(2,1)} %bitcast.28, s32[1024]{0:T(1024)S(1)} %pad_clamp_fusion), kind=kCustom, calls=%fused_computation.3 | custom fusion | bytes 4196352 | tf_op jit(solution)/shard_map/jit(_take)/gather | solution.py:142
  576.2 2.2 gather.31
  578.5 3.0 fusion.1
  581.5 1.1 copy.100
  582.6 69.9 %all-reduce.5.cloned.1.call-done = bf16[128,2048]{1,0:T(8,128)(2,1)} async-done(((bf16[128,2048]{1,0:T(8,128)(2,1)}), bf16[128,2048]{1,0:T(8,128)(2,1)}) %all-reduce.5.cloned.1.call-update) | async-done | bytes 524304 | tf_op jit(solution)/shard_map/psum | solution.py:145
  652.5 1.2 add_convert_fusion
  653.7 0.1 copy.93
  653.9 0.1 constant_dynamic-slice_fusion
  654.0 0.6 copy.101
  (59 shorter events, 1.1 us)
Async XLA Ops:
  6.5 361.5 %copy-start = (bf16[1,176,2048]{2,1,0:T(8,128)(2,1)S(1)}, bf16[1,176,2048]{2,1,0:T(8,128)(2,1)}, u32[]{:S(2)}) copy-start(bf16[1,176,2048]{2,1,0:T(8,128)(2,1)} %param.21) | copy-start | bytes 2162692
  6.5 24.6 %copy-start.6 = (s32[128,4]{0,1:T(4,128)S(1)}, s32[128,4]{0,1:T(4,128)}, u32[]{:S(2)}) copy-start(s32[128,4]{0,1:T(4,128)} %param.26) | copy-start | bytes 6148
  6.5 26.6 %copy-start.5 = (bf16[128,384]{1,0:T(8,128)(2,1)S(1)}, bf16[128,384]{1,0:T(8,128)(2,1)}, u32[]{:S(2)}) copy-start(bf16[128,384]{1,0:T(8,128)(2,1)} %param.14) | copy-start | bytes 294916
  6.5 26.9 %copy-start.12 = (s32[1,1,4]{2,1,0:T(1,128)S(1)}, s32[1,1,4]{2,1,0:T(1,128)}, u32[]{:S(2)}) copy-start(s32[1,1,4]{2,1,0:T(1,128)} %param.23) | copy-start | bytes 52
  6.5 31.1 %copy-start.8 = (s32[1,1,128]{2,1,0:T(1,128)S(1)}, s32[1,1,128]{2,1,0:T(1,128)}, u32[]{:S(2)}) copy-start(s32[1,1,128]{2,1,0:T(1,128)} %param.22) | copy-start | bytes 1540
  11.0 67.2 %copy-start.4 = (bf16[128,2048]{1,0:T(8,128)(2,1)S(1)}, bf16[128,2048]{1,0:T(8,128)(2,1)}, u32[]{:S(2)}) copy-start(bf16[128,2048]{1,0:T(8,128)(2,1)} %param.17) | copy-start | bytes 1572868
  12.4 62.7 %all-to-all-start = ((bf16[64,3,8,256]{3,2,1,0:T(8,128)(2,1)}), bf16[64,3,8,256]{3,2,1,0:T(8,128)(2,1)S(1)}, u32[]{:S(2)}, u32[]{:S(2)}) async-start(bf16[64,3,8,256]{3,2,1,0:T(8,128)(2,1)} %select_select_fusion.1), calls=%async_computation | async-start | bytes 1572864 | tf_op jit(solution)/shard_map/all_to_all | solution.py:90
  31.1 118.3 %all-reduce.3.cloned.1.call-start = ((), (), s32[]{:S(2)}) async-start(), calls=%async_computation.3 | async-start | bytes 2097152 | tf_op jit(solution)/shard_map/psum | solution.py:134
  33.8 115.6 %copy-start.2 = (bf16[128,2048]{1,0:T(8,128)(2,1)S(1)}, bf16[128,2048]{1,0:T(8,128)(2,1)}, u32[]{:S(2)}) copy-start(bf16[128,2048]{1,0:T(8,128)(2,1)} %param.16) | copy-start | bytes 1572868
  75.7 75.1 %copy-start.7 = (f32[2048]{0:T(1024)S(1)}, f32[2048]{0:T(1024)}, u32[]{:S(2)}) copy-start(f32[2048]{0:T(1024)} %param.18) | copy-start | bytes 24580
  160.8 205.6 %copy-start.10 = (bf16[1,2048,176]{1,2,0:T(8,128)(2,1)S(1)}, bf16[1,2048,176]{1,2,0:T(8,128)(2,1)}, u32[]{:S(2)}) copy-start(bf16[1,2048,176]{1,2,0:T(8,128)(2,1)} %param.19) | copy-start | bytes 2162692
  364.5 2.0 copy-start.3
  364.5 3.5 copy-start.11
  374.9 7.1 %copy-start.9 = (f32[128,4]{0,1:T(4,128)S(1)}, f32[128,4]{0,1:T(4,128)}, u32[]{:S(2)}) copy-start(f32[128,4]{0,1:T(4,128)} %param.27) | copy-start | bytes 6148
  374.9 194.2 %all-to-all-start.2 = ((bf16[64,16,2048]{2,1,0:T(8,128)(2,1)}), bf16[64,16,2048]{2,1,0:T(8,128)(2,1)}, u32[]{:S(2)}, u32[]{:S(2)}) async-start(bf16[64,16,2048]{2,1,0:T(8,128)(2,1)} %bitcast.86), calls=%async_computation.2 | async-start | bytes 8388608 | tf_op jit(solution)/shard_map/all_to_all | solution.py:140
  381.2 271.3 %all-reduce.5.cloned.1.call-start = ((), (), s32[]{:S(2)}) async-start(), calls=%async_computation.4 | async-start | bytes 1048576 | tf_op jit(solution)/shard_map/psum | solution.py:145
  578.5 74.0 %copy-start.1 = (f32[128,2048]{1,0:T(8,128)S(1)}, f32[128,2048]{1,0:T(8,128)}, u32[]{:S(2)}) copy-start(f32[128,2048]{1,0:T(8,128)} %all-reduce.3.cloned.1.call-done) | copy-start | bytes 3145732
Sparse Core Ops, SparseCore 0:
  79.9 69.3 all-reduce.2
  582.8 69.7 all-reduce.4
where the time goes:
time: 662 us; the launch traced here: 661 us
  waiting for transfers between devices  362 us (55%)
  blocking collectives  204 us (31%)
  local copies, waits for them, and re-layouts  25.6 us (4%)
  starting transfers between devices  25.1 us (4%)
  other arithmetic  17.9 us (3%)
  between operations  13.8 us (2%)
  matrix products  13.2 us (2%)
    all_to_all x1, blocking collectives, local(): lax.all_to_all(outgoing, 'dp', split_axis=0, concat_axis=0, tiled=True)  204 us
    all_to_all x1, waiting for transfers between devices, local(): lax.all_to_all(produced, 'dp', split_axis=0, concat_axis=0, tiled=True)  187 us
    psum x1, waiting for transfers between devices, local(): lax.psum(weighted.astype(jnp.bfloat16), ('section', 'mp'))  69.9 us
    psum x1, waiting for transfers between devices, local(): mixed_in = stream + lax.psum(projected, ('section', 'mp'))  68.3 us
    all_to_all x1, waiting for transfers between devices, local(): lax.all_to_all(chosen, 'dp', split_axis=0, concat_axis=0, tiled=True)  37.1 us
    all_to_all x1, starting transfers between devices, local(): lax.all_to_all(chosen, 'dp', split_axis=0, concat_axis=0, tiled=True)  18.7 us
  transfers between devices with their start and end apart: 4, of which 4 were waited for; matrix products, arithmetic and copies ran while one was open for 1% of the time, Pallas kernels for 0%

commit v1 on v0

--- a/solution.py
+++ b/solution.py
@@ -131,7 +131,7 @@
     flat_slot = (quarter_rank + jnp.arange(shards, dtype=jnp.int32)[:, None] * quarter_cap).reshape(
         -1
     )
-    mixed_in = stream + lax.psum(projected, ("section", "mp"))
+    mixed_in = stream + lax.psum(lax.psum(projected, "mp"), "section")
     normed = normalize(mixed_in, moe_gain)
     source, filled = slot_table(flat_ids, flat_slot, groups, capacity)
     outgoing = dispatch_rows(normed, source, filled)

time: 662 us -> 693 us (1.047)
  waiting for transfers between devices: 362 us -> 390 us
    psum x1 -> x2, waiting for transfers between devices: 68.3 us -> 93.1 us  [local(): mixed_in = stream + lax.psum(lax.psum(projected, 'mp'), 'section')]
  transfers between devices with their start and end apart: 4 -> 5, of which waited for: 4 -> 5; matrix products, arithmetic and copies ran while one was open for 1% -> 1% of each run, Pallas kernels for 0% -> 0%
where the time goes in v1:
time: 693 us; the launch traced here: 692 us
  waiting for transfers between devices  390 us (56%)
  blocking collectives  206 us (30%)
  local copies, waits for them, and re-layouts  25.6 us (4%)
  starting transfers between devices  25.1 us (4%)
  other arithmetic  17.9 us (3%)
  matrix products  14.3 us (2%)
  between operations  13.5 us (2%)
    all_to_all x1, blocking collectives, local(): lax.all_to_all(outgoing, 'dp', split_axis=0, concat_axis=0, tiled=True)  206 us
    all_to_all x1, waiting for transfers between devices, local(): lax.all_to_all(produced, 'dp', split_axis=0, concat_axis=0, tiled=True)  188 us
    psum x2, waiting for transfers between devices, local(): mixed_in = stream + lax.psum(lax.psum(projected, 'mp'), 'section')  93.1 us
    psum x1, waiting for transfers between devices, local(): lax.psum(weighted.astype(jnp.bfloat16), ('section', 'mp'))  67.7 us
    all_to_all x1, waiting for transfers between devices, local(): lax.all_to_all(chosen, 'dp', split_axis=0, concat_axis=0, tiled=True)  40.4 us
    all_to_all x1, starting transfers between devices, local(): lax.all_to_all(chosen, 'dp', split_axis=0, concat_axis=0, tiled=True)  18.7 us
  transfers between devices with their start and end apart: 5, of which 5 were waited for; matrix products, arithmetic and copies ran while one was open for 1% of the time, Pallas kernels for 0%

profile of v1, /device:TPU:8, one launch (start us, length us, event | category | flops | bytes accessed | tf_op | source)
XLA Modules:
  0.0 692.3 jit_solution(5267021118632527402)
XLA Ops:
  6.5 0.9 broadcast_compare_fusion.1
  7.4 0.2 reduce_window_sum.29
  7.7 0.9 select_reduce_fusion
  8.6 0.1 copy.73
  8.7 0.2 fusion.36
  8.8 0.1 reshape.389
  9.0 0.1 copy.72
  9.1 0.1 copy.71
  9.2 1.8 gather_fusion
  11.0 1.3 select_select_fusion.1
  12.3 18.7 %all-to-all-start = ((bf16[64,3,8,256]{3,2,1,0:T(8,128)(2,1)}), bf16[64,3,8,256]{3,2,1,0:T(8,128)(2,1)S(1)}, u32[]{:S(2)}, u32[]{:S(2)}) async-start(bf16[64,3,8,256]{3,2,1,0:T(8,128)(2,1)} %select_select_fusion.1), calls=%async_computation | async-start | bytes 1572864 | tf_op jit(solution)/shard_map/all_to_all | solution.py:90
  31.1 0.7 fusion.43
  31.8 0.2 convert_reduce_fusion
  32.0 0.7 compare_and_fusion.3
  32.7 0.1 broadcast_in_dim.123
  32.8 0.1 copy.74
  33.0 0.1 copy.76
  33.1 0.2 reduce-window.8
  33.3 0.1 convert_reduce_fusion.1
  33.5 0.1 eq.135
  33.6 0.1 copy.75
  33.7 0.7 fusion.42
  34.4 0.1 fusion.37
  34.4 0.1 broadcast_compare_fusion
  34.6 40.4 %all-to-all-done = bf16[64,3,8,256]{3,2,1,0:T(8,128)(2,1)S(1)} async-done(((bf16[64,3,8,256]{3,2,1,0:T(8,128)(2,1)}), bf16[64,3,8,256]{3,2,1,0:T(8,128)(2,1)S(1)}, u32[]{:S(2)}, u32[]{:S(2)}) %all-to-all-start) | async-done | bytes 786464 | tf_op jit(solution)/shard_map/all_to_all | solution.py:90
  75.0 0.6 gather_fusion.1
  75.7 1.8 broadcast_select_fusion
  77.5 0.4 fusion.50
  77.9 0.2 fusion.52
  78.1 0.1 fusion.22
  78.3 1.6 fusion.8
  79.9 0.1 copy.78
  80.0 0.1 eq.143
  80.1 0.1 eq.147
  80.2 0.1 copy.79
  80.3 1.4 fusion.53
  82.0 50.8 %all-reduce.4.cloned.1.call-done = f32[128,2048]{1,0:T(8,128)} async-done(((f32[128,2048]{1,0:T(8,128)}), f32[128,2048]{1,0:T(8,128)}) %all-reduce.4.cloned.1.call-update) | async-done | bytes 1048592 | tf_op jit(solution)/shard_map/psum | solution.py:134
  132.8 1.2 fusion
  134.0 0.1 reshape.398
  134.1 1.2 and_reduce_fusion
  135.3 42.3 %all-reduce.6.cloned.1.call-done = f32[128,2048]{1,0:T(8,128)} async-done(((f32[128,2048]{1,0:T(8,128)}), f32[128,2048]{1,0:T(8,128)}) %all-reduce.6.cloned.1.call-update) | async-done | bytes 1048592 | tf_op jit(solution)/shard_map/psum | solution.py:134
  177.6 1.4 multiply_reduce_fusion
  179.1 1.4 multiply_convert_fusion
  180.5 6.0 gather_fusion.2
  186.5 2.6 select_select_fusion
  189.1 206.1 %all_to_all.15 = bf16[64,16,2048]{2,1,0:T(8,128)(2,1)S(1)} all-to-all(bf16[64,16,2048]{2,1,0:T(8,128)(2,1)S(1)} %select_select_fusion), channel_id=1, replica_groups=mesh['section'=2,'dp'=64,'mp'=4] {'dp'}, dimensions={0} | all-to-all | bytes 8388608 | tf_op jit(solution)/shard_map/all_to_all | solution.py:138
  395.2 2.0 copy-done.3
  397.2 2.4 fusion.14
  399.6 7.0 %convolution_convert_fusion = bf16[1024,2048]{1,0:T(8,128)(2,1)} fusion(bf16[1024,2048]{1,0:T(8,128)(2,1)} %bitcast.88, bf16[1,176,2048]{2,1,0:T(8,128)(2,1)S(1)} %copy-done, bf16[1,2048,176]{1,2,0:T(8,128)(2,1)S(1)} %copy-done.11, f32[1024,176]{0,1:T(8,128)} %fusion.14), kind=kOutput, calls=%fused_computation.5 | convolution fusion | flops 1479573504 | bytes 10551296 | tf_op jit(solution)/shard_map/dot_general | solution.py:24
  406.7 6.3 all-to-all-start.2
  413.2 0.1 copy.85
  413.3 0.1 mul.112
  413.6 0.1 copy.82
  413.8 0.2 copy.87
  414.0 188.4 %all-to-all-done.2 = bf16[64,16,2048]{2,1,0:T(8,128)(2,1)} async-done(((bf16[64,16,2048]{2,1,0:T(8,128)(2,1)}), bf16[64,16,2048]{2,1,0:T(8,128)(2,1)}, u32[]{:S(2)}, u32[]{:S(2)}) %all-to-all-start.2) | async-done | bytes 4194336 | tf_op jit(solution)/shard_map/all_to_all | solution.py:140
  602.4 7.1 %gather_fusion.3 = bf16[512,2048]{1,0:T(8,128)(2,1)S(1)} fusion(bf16[1024,2048]{1,0:T(8,128)(2,1)} %bitcast.28, s32[1024]{0:T(1024)S(1)} %pad_clamp_fusion), kind=kCustom, calls=%fused_computation.3 | custom fusion | bytes 4196352 | tf_op jit(solution)/shard_map/jit(_take)/gather | solution.py:142
  609.5 2.2 gather.31
  611.7 3.0 fusion.1
  614.7 1.1 copy.100
  615.9 67.7 %all-reduce.8.cloned.1.call-done = bf16[128,2048]{1,0:T(8,128)(2,1)} async-done(((bf16[128,2048]{1,0:T(8,128)(2,1)}), bf16[128,2048]{1,0:T(8,128)(2,1)}) %all-reduce.8.cloned.1.call-update) | async-done | bytes 524304 | tf_op jit(solution)/shard_map/psum | solution.py:145
  683.6 1.2 add_convert_fusion
  684.8 0.1 copy.93
  685.0 0.1 constant_dynamic-slice_fusion
  685.1 0.6 copy.101
  (62 shorter events, 1.2 us)
Async XLA Ops:
  6.5 393.1 %copy-start = (bf16[1,176,2048]{2,1,0:T(8,128)(2,1)S(1)}, bf16[1,176,2048]{2,1,0:T(8,128)(2,1)}, u32[]{:S(2)}) copy-start(bf16[1,176,2048]{2,1,0:T(8,128)(2,1)} %param.21) | copy-start | bytes 2162692
  6.5 26.3 %copy-start.5 = (bf16[128,384]{1,0:T(8,128)(2,1)S(1)}, bf16[128,384]{1,0:T(8,128)(2,1)}, u32[]{:S(2)}) copy-start(bf16[128,384]{1,0:T(8,128)(2,1)} %param.14) | copy-start | bytes 294916
  6.5 26.6 %copy-start.12 = (s32[1,1,4]{2,1,0:T(1,128)S(1)}, s32[1,1,4]{2,1,0:T(1,128)}, u32[]{:S(2)}) copy-start(s32[1,1,4]{2,1,0:T(1,128)} %param.23) | copy-start | bytes 52
  6.5 27.8 %copy-start.8 = (s32[1,1,128]{2,1,0:T(1,128)S(1)}, s32[1,1,128]{2,1,0:T(1,128)}, u32[]{:S(2)}) copy-start(s32[1,1,128]{2,1,0:T(1,128)} %param.22) | copy-start | bytes 1540
  11.0 67.2 %copy-start.4 = (bf16[128,2048]{1,0:T(8,128)(2,1)S(1)}, bf16[128,2048]{1,0:T(8,128)(2,1)}, u32[]{:S(2)}) copy-start(bf16[128,2048]{1,0:T(8,128)(2,1)} %param.17) | copy-start | bytes 1572868
  12.3 62.7 %all-to-all-start = ((bf16[64,3,8,256]{3,2,1,0:T(8,128)(2,1)}), bf16[64,3,8,256]{3,2,1,0:T(8,128)(2,1)S(1)}, u32[]{:S(2)}, u32[]{:S(2)}) async-start(bf16[64,3,8,256]{3,2,1,0:T(8,128)(2,1)} %select_select_fusion.1), calls=%async_computation | async-start | bytes 1572864 | tf_op jit(solution)/shard_map/all_to_all | solution.py:90
  31.1 48.8 %copy-start.6 = (s32[128,4]{0,1:T(4,128)S(1)}, s32[128,4]{0,1:T(4,128)}, u32[]{:S(2)}) copy-start(s32[128,4]{0,1:T(4,128)} %param.26) | copy-start | bytes 6148
  31.1 101.7 %all-reduce.4.cloned.1.call-start = ((), (), s32[]{:S(2)}) async-start(), calls=%async_computation.3 | async-start | bytes 2097152 | tf_op jit(solution)/shard_map/psum | solution.py:134
  75.7 101.9 %copy-start.2 = (bf16[128,2048]{1,0:T(8,128)(2,1)S(1)}, bf16[128,2048]{1,0:T(8,128)(2,1)}, u32[]{:S(2)}) copy-start(bf16[128,2048]{1,0:T(8,128)(2,1)} %param.16) | copy-start | bytes 1572868
  77.8 101.2 %copy-start.7 = (f32[2048]{0:T(1024)S(1)}, f32[2048]{0:T(1024)}, u32[]{:S(2)}) copy-start(f32[2048]{0:T(1024)} %param.18) | copy-start | bytes 24580
  79.9 97.8 %all-reduce.6.cloned.1.call-start = ((), (), s32[]{:S(2)}) async-start(), calls=%async_computation.4 | async-start | bytes 2097152 | tf_op jit(solution)/shard_map/psum | solution.py:134
  189.1 208.1 %copy-start.10 = (bf16[1,2048,176]{1,2,0:T(8,128)(2,1)S(1)}, bf16[1,2048,176]{1,2,0:T(8,128)(2,1)}, u32[]{:S(2)}) copy-start(bf16[1,2048,176]{1,2,0:T(8,128)(2,1)} %param.19) | copy-start | bytes 2162692
  395.2 2.0 copy-start.3
  395.2 4.4 copy-start.11
  406.7 7.1 %copy-start.9 = (f32[128,4]{0,1:T(4,128)S(1)}, f32[128,4]{0,1:T(4,128)}, u32[]{:S(2)}) copy-start(f32[128,4]{0,1:T(4,128)} %param.27) | copy-start | bytes 6148
  406.7 195.7 %all-to-all-start.2 = ((bf16[64,16,2048]{2,1,0:T(8,128)(2,1)}), bf16[64,16,2048]{2,1,0:T(8,128)(2,1)}, u32[]{:S(2)}, u32[]{:S(2)}) async-start(bf16[64,16,2048]{2,1,0:T(8,128)(2,1)} %bitcast.86), calls=%async_computation.2 | async-start | bytes 8388608 | tf_op jit(solution)/shard_map/all_to_all | solution.py:140
  413.0 270.7 %all-reduce.8.cloned.1.call-start = ((), (), s32[]{:S(2)}) async-start(), calls=%async_computation.5 | async-start | bytes 1048576 | tf_op jit(solution)/shard_map/psum | solution.py:145
  611.7 71.9 %copy-start.1 = (f32[128,2048]{1,0:T(8,128)S(1)}, f32[128,2048]{1,0:T(8,128)}, u32[]{:S(2)}) copy-start(f32[128,2048]{1,0:T(8,128)} %all-reduce.6.cloned.1.call-done) | copy-start | bytes 3145732
Sparse Core Ops, SparseCore 0:
  80.0 52.7 all-reduce.3
  135.9 41.6 all-reduce.5
  616.0 67.5 all-reduce.7
